TPU v7x, 128 devices: a whole 4x4x4 slice. The times are simulated.
128 devices in a mesh: sample: 8 (over z_lo, y), feat: 16 (over x, z_hi, core).
Axes of the slice: x: 4, y: 4, z: 4 (z_hi: 2, z_lo: 2; z = z_hi * 2 + z_lo), core: 2. Of those that a mesh axis runs over, the one named last changes fastest.
Arguments:
- view_a: bfloat16 [1024, 16384], P('sample', 'feat'), may hold values from -60 to 60
- view_b: bfloat16 [1024, 16384], P('sample', 'feat'), may hold values from -60 to 60
Outputs:
- loss: float32 [], replicated
- grad_a: bfloat16 [1024, 16384], P('sample', 'feat')
- grad_b: bfloat16 [1024, 16384], P('sample', 'feat')
All inputs are finite; a program needn't handle non-finite values.
Results may differ from a plain program's by a relative error of at most 0.02.
Values may be sent and summed in bfloat16 or wider, within the bound.
No kernel may reach another device: no remote copies, remote signals or barrier semaphores. Data moves between devices by JAX's collectives and lax.ppermute only.
A program may use at most 64 MiB of HBM per device.

v0:
```python
import jax
import jax.numpy as jnp
from jax import lax
from jax.sharding import PartitionSpec as P

EPSILON = 1e-05
OFF_WEIGHT = 0.0051


def body(view_a, view_b):
    rows_dev, cols_dev = view_a.shape
    groups = lax.axis_size("sample")
    blocks = lax.axis_size("feat")
    total_rows = rows_dev * groups
    sub_width = cols_dev // groups
    inv_rows = 1.0 / total_rows
    sample_id = lax.axis_index("sample")
    feat_id = lax.axis_index("feat")
    float_a = view_a.astype(jnp.float32)
    float_b = view_b.astype(jnp.float32)
    moment_sums = lax.psum(
        (
            jnp.sum(float_a, axis=0),
            jnp.sum(float_a * float_a, axis=0),
            jnp.sum(float_b, axis=0),
            jnp.sum(float_b * float_b, axis=0),
        ),
        "sample",
    )
    mean_a = moment_sums[0] * inv_rows
    scale_a = lax.rsqrt(moment_sums[1] * inv_rows - mean_a * mean_a + EPSILON)
    mean_b = moment_sums[2] * inv_rows
    scale_block_b = lax.rsqrt(moment_sums[3] * inv_rows - mean_b * mean_b + EPSILON)
    local_a = ((float_a - mean_a) * scale_a).astype(jnp.bfloat16)
    source_b = ((float_b - mean_b) * scale_block_b).astype(jnp.bfloat16)
    scale_b = lax.dynamic_slice_in_dim(scale_block_b, sample_id * sub_width, sub_width)
    norm_a = lax.all_gather(local_a, "sample", axis=0, tiled=True)
    row_index = jnp.arange(cols_dev, dtype=jnp.int32)
    wide_b = lax.all_gather(source_b, "feat", axis=1, tiled=True)
    arranged = (
        wide_b.reshape(rows_dev, blocks, groups, sub_width)
        .transpose(0, 2, 1, 3)
        .reshape(rows_dev, blocks * cols_dev)
    )
    moved_b = lax.all_to_all(arranged, "sample", split_axis=1, concat_axis=0, tiled=True)
    own_b = lax.dynamic_slice_in_dim(moved_b, feat_id * sub_width, sub_width, 1)
    panel_width = moved_b.shape[1]
    correlation = (
        lax.dot_general(
            norm_a, moved_b, (((0,), (0,)), ((), ())), preferred_element_type=jnp.float32
        )
        * inv_rows
    )
    local_cols = jnp.arange(panel_width, dtype=jnp.int32)
    owner_block = local_cols // sub_width
    offset = local_cols % sub_width
    on_diagonal = (owner_block[None, :] == feat_id) & (
        offset[None, :] + sample_id * sub_width == row_index[:, None]
    )
    missing = 1.0 - correlation
    piece_loss = jnp.sum(
        jnp.where(on_diagonal, missing * missing, OFF_WEIGHT * correlation * correlation)
    )
    factor = jnp.where(on_diagonal, correlation - 1.0, OFF_WEIGHT * correlation).astype(
        jnp.bfloat16
    )
    grad_rows = lax.dot_general(
        moved_b, factor, (((1,), (1,)), ((), ())), preferred_element_type=jnp.float32
    )
    folded = (piece_loss, grad_rows, factor)
    loss_sum, grad_rows, factor_tile = folded
    row_grad = lax.psum_scatter(
        grad_rows.astype(jnp.bfloat16), "sample", scatter_dimension=0, tiled=True
    ).astype(jnp.float32)
    float_local = local_a.astype(jnp.float32)
    moments = lax.psum(
        (jnp.sum(row_grad, axis=0), jnp.sum(row_grad * float_local, axis=0)), "sample"
    )
    grad_a = (
        scale_a * (row_grad - moments[0] * inv_rows - float_local * (moments[1] * inv_rows))
    ).astype(jnp.bfloat16)
    col_grad = lax.psum_scatter(
        lax.dot_general(
            factor_tile, norm_a, (((0,), (1,)), ((), ())), preferred_element_type=jnp.float32
        ).astype(jnp.bfloat16),
        "feat",
        scatter_dimension=0,
        tiled=True,
    ).astype(jnp.float32)
    own_t = own_b.T.astype(jnp.float32)
    mean_grad = jnp.mean(col_grad, axis=1, keepdims=True)
    mean_cross = jnp.mean(col_grad * own_t, axis=1, keepdims=True)
    grad_b_t = (scale_b[:, None] * (col_grad - mean_grad - own_t * mean_cross)).astype(jnp.bfloat16)
    returned = lax.all_to_all(grad_b_t, "sample", split_axis=1, concat_axis=0, tiled=True)
    grad_b = returned.T
    loss = lax.psum(loss_sum, ("sample", "feat")) / (cols_dev * blocks)
    return (loss, grad_a, grad_b)


def solution(mesh):
    in_specs = (P("sample", "feat"), P("sample", "feat"))
    out_specs = (P(), P("sample", "feat"), P("sample", "feat"))
    return jax.shard_map(body, mesh=mesh, in_specs=in_specs, out_specs=out_specs, check_vma=False)
```

profile of v0, /device:TPU:0, one launch (start us, length us, event | category | flops | bytes accessed | tf_op | source)
XLA Modules:
  0.0 370.2 jit_solution(4005084618769182151)
XLA Ops:
  7.2 0.0 all-gather.5.cloned.1.call-start
  7.2 1.2 convert_reduce_fusion.2
  8.4 34.9 %all-reduce.1 = (f32[1024]{0:T(1024)S(1)}, f32[1024]{0:T(1024)S(1)}, f32[1024]{0:T(1024)S(1)}, f32[1024]{0:T(1024)S(1)}) all-reduce(f32[1024]{0:T(1024)S(1)} %get-tuple-element.23, f32[1024]{0:T(1024)S(1)} %get-tuple-element.24, f32[1024]{0:T(1024)S(1)} %get-tuple-element.8, ...), channel_id=1, replica_groups=mesh['sample'=8,'feat'=16] {'sample'}, use_global_device_ids=true, to_apply=%region_3.0 | all-reduce | flops 4096 | bytes 32768 | tf_op jit(solution)/shard_map/psum | solution.py:21
  43.4 1.7 fusion.8
  45.1 0.0 all-gather.5.cloned.1.call-update
  45.1 0.0 all-gather.3.cloned.1.call-start
  45.2 1.7 fusion.5
  46.9 0.0 all-gather.3.cloned.1.call-update
  46.9 53.7 %all-gather.5.cloned.1.call-done = bf16[128,16384]{1,0:T(8,128)(2,1)} async-done(((bf16[128,1024]{1,0:T(8,128)(2,1)}), bf16[128,16384]{1,0:T(8,128)(2,1)}) %all-gather.5.cloned.1.call-update) | async-done | bytes 4194320 | tf_op jit(solution)/shard_map/all_gather | solution.py:39
  100.6 5.4 %copy.13 = bf16[16,8,128,128]{3,2,1,0:T(8,128)(2,1)} copy(bf16[16,8,128,128]{3,1,2,0:T(8,128)(2,1)} %bitcast.43) | data formatting | bytes 8388608
  106.0 6.9 %copy.7 = bf16[128,16,8,128]{0,3,1,2:T(8,128)(2,1)} copy(bf16[128,16,8,128]{3,2,1,0:T(8,128)(2,1)} %bitcast.42) | data formatting | bytes 8388608 | tf_op jit(solution)/shard_map/reshape | solution.py:41
  112.9 4.6 %all-to-all-start = ((bf16[128,8,2048]{0,2,1:T(8,128)(2,1)}), bf16[128,8,2048]{0,2,1:T(8,128)(2,1)}, u32[]{:S(2)}, u32[]{:S(2)}) async-start(bf16[128,8,2048]{0,2,1:T(8,128)(2,1)} %bitcast.41), calls=%async_computation | async-start | bytes 8388608 | tf_op jit(solution)/shard_map/all_to_all | solution.py:45
  117.5 0.0 reduce-scatter.3.cloned.1.call-start
  117.6 80.9 %all-gather.3.cloned.1.call-done = bf16[1024,1024]{1,0:T(8,128)(2,1)} async-done(((bf16[128,1024]{1,0:T(8,128)(2,1)}), bf16[1024,1024]{1,0:T(8,128)(2,1)}) %all-gather.3.cloned.1.call-update) | async-done | bytes 2097168 | tf_op jit(solution)/shard_map/all_gather | solution.py:37
  198.5 0.0 all-to-all-done
  198.5 9.5 %select_reduce_fusion = (f32[]{:T(128)}, f32[1024,2048]{1,0:T(8,128)S(1)}) fusion(s32[2048]{0:T(1024)S(1)} %fusion.23, pred[2048]{0:T(1024)(128)(4,1)S(1)} %fusion.22, bf16[1024,1024]{1,0:T(8,128)(2,1)} %all-gather.3.cloned.1.call-done, bf16[128,8,2048]{0,2,1:T(8,128)(2,1)} %all-to-all-done), kind=kOutput, calls=%fused_computation.1 | convolution fusion | flops 4313841664 | bytes 14690308 | tf_op jit(solution)/shard_map/dot_general | solution.py:49
  208.0 0.0 copy-start.2
  208.0 3.2 copy-done.2
  211.2 0.0 copy-start.1
  211.2 8.4 %convolution_convert_fusion.1 = bf16[1024,1024]{1,0:T(8,128)(2,1)} fusion(f32[1024,2048]{1,0:T(8,128)S(1)} %get-tuple-element.22, s32[2048]{0:T(1024)S(1)} %fusion.23, pred[2048]{0:T(1024)(128)(4,1)S(1)} %fusion.22, bf16[128,8,2048]{0,2,1:T(8,128)(2,1)} %all-to-all-done), kind=kOutput, calls=%fused_computation.6 | convolution fusion | flops 4310695936 | bytes 14690304 | tf_op jit(solution)/shard_map/dot_general | solution.py:67
  219.7 0.0 reduce-scatter.3.cloned.1.call-update
  219.7 0.0 reduce-scatter.5.cloned.1.call-start
  219.7 0.0 copy-done.1
  219.7 12.0 %convolution_convert_fusion = bf16[2048,1024]{1,0:T(8,128)(2,1)} fusion(bf16[1024,1024]{1,0:T(8,128)(2,1)S(1)} %copy-done.1, f32[1024,2048]{1,0:T(8,128)} %copy-done.2, s32[2048]{0:T(1024)S(1)} %fusion.23, pred[2048]{0:T(1024)(128)(4,1)S(1)} %fusion.22), kind=kOutput, calls=%fused_computation.5 | convolution fusion | flops 4311744512 | bytes 14690304 | tf_op jit(solution)/shard_map/dot_general | solution.py:83
  231.7 0.0 reduce-scatter.5.cloned.1.call-update
  231.7 0.1 dynamic_slice.6
  231.8 65.5 %psum.53 = f32[]{:T(128)} all-reduce(f32[]{:T(128)} %get-tuple-element.21), channel_id=1, replica_groups=mesh['sample'=8,'feat'=16] {'sample','feat'}, use_global_device_ids=true, to_apply=%region_9.10 | all-reduce | flops 1 | bytes 8 | tf_op jit(solution)/shard_map/psum | solution.py:96
  298.0 0.0 copy-start
  298.0 4.8 %copy_bitcast_fusion = bf16[1024,2048]{0,1:T(8,128)(2,1)} fusion(bf16[128,8,2048]{0,2,1:T(8,128)(2,1)} %all-to-all-done), kind=kLoop, calls=%fused_computation.4 | loop fusion | bytes 8388608 | tf_op jit(solution)/shard_map/all_to_all | solution.py:45
  302.8 0.0 reduce-scatter.3.cloned.1.call-done
  302.8 0.0 copy-done
  302.8 1.1 convert_reduce_fusion.1
  303.9 17.7 %all-reduce = (f32[1024]{0:T(1024)S(1)}, f32[1024]{0:T(1024)S(1)}) all-reduce(f32[1024]{0:T(1024)S(1)} %get-tuple-element.6, f32[1024]{0:T(1024)S(1)} %get-tuple-element.5), channel_id=1, replica_groups=mesh['sample'=8,'feat'=16] {'sample'}, use_global_device_ids=true, to_apply=%region_14.15 | all-reduce | flops 2048 | bytes 16384 | tf_op jit(solution)/shard_map/psum | solution.py:76
  321.7 25.1 %reduce-scatter.5.cloned.1.call-done = bf16[128,1024]{1,0:T(8,128)(2,1)} async-done(((bf16[2048,1024]{1,0:T(8,128)(2,1)}), bf16[128,1024]{1,0:T(8,128)(2,1)}) %reduce-scatter.5.cloned.1.call-update) | async-done | bytes 262160 | tf_op jit(solution)/shard_map/reduce_scatter | solution.py:82
  346.8 1.2 convert_reduce_fusion
  348.0 2.0 copy_bitcast_fusion.1
  350.0 4.4 %all-to-all-start.1 = ((bf16[128,8,128]{2,0,1:T(8,128)(2,1)}), bf16[128,8,128]{2,0,1:T(8,128)(2,1)S(1)}, u32[]{:S(2)}, u32[]{:S(2)}) async-start(bf16[128,8,128]{2,0,1:T(8,128)(2,1)} %copy_bitcast_fusion.1), calls=%async_computation.3 | async-start | bytes 524288 | tf_op jit(solution)/shard_map/all_to_all | solution.py:94
  354.4 1.8 fusion.3
  356.2 5.5 %all-to-all-done.1 = bf16[128,8,128]{2,0,1:T(8,128)(2,1)S(1)} async-done(((bf16[128,8,128]{2,0,1:T(8,128)(2,1)}), bf16[128,8,128]{2,0,1:T(8,128)(2,1)S(1)}, u32[]{:S(2)}, u32[]{:S(2)}) %all-to-all-start.1) | async-done | bytes 262176 | tf_op jit(solution)/shard_map/all_to_all | solution.py:94
  361.7 0.8 copy.10
  (8 shorter events, 0.1 us)
Async XLA Ops:
  7.2 93.5 %all-gather.5.cloned.1.call-start = ((), (), s32[]{:S(2)}) async-start(), calls=%async_computation.5 | async-start | bytes 4456448 | tf_op jit(solution)/shard_map/all_gather | solution.py:39
  45.1 153.4 %all-gather.3.cloned.1.call-start = ((), (), s32[]{:S(2)}) async-start(), calls=%async_computation.4 | async-start | bytes 2359296 | tf_op jit(solution)/shard_map/all_gather | solution.py:37
  112.9 85.6 %all-to-all-start = ((bf16[128,8,2048]{0,2,1:T(8,128)(2,1)}), bf16[128,8,2048]{0,2,1:T(8,128)(2,1)}, u32[]{:S(2)}, u32[]{:S(2)}) async-start(bf16[128,8,2048]{0,2,1:T(8,128)(2,1)} %bitcast.41), calls=%async_computation | async-start | bytes 8388608 | tf_op jit(solution)/shard_map/all_to_all | solution.py:45
  117.5 185.3 %reduce-scatter.3.cloned.1.call-start = ((), (), s32[]{:S(2)}) async-start(), calls=%async_computation.6 | async-start | bytes 2359296 | tf_op jit(solution)/shard_map/reduce_scatter | solution.py:72
  208.0 3.2 copy-start.2
  211.2 8.5 %copy-start.1 = (bf16[1024,1024]{1,0:T(8,128)(2,1)S(1)}, bf16[1024,1024]{1,0:T(8,128)(2,1)}, u32[]{:S(2)}) copy-start(bf16[1024,1024]{1,0:T(8,128)(2,1)} %all-gather.3.cloned.1.call-done) | copy-start | bytes 6291460
  219.7 127.1 %reduce-scatter.5.cloned.1.call-start = ((), (), s32[]{:S(2)}) async-start(), calls=%async_computation.7 | async-start | bytes 4456448 | tf_op jit(solution)/shard_map/reduce_scatter | solution.py:82
  298.0 4.8 %copy-start = (bf16[128,1024]{1,0:T(8,128)(2,1)S(1)}, bf16[128,1024]{1,0:T(8,128)(2,1)}, u32[]{:S(2)}) copy-start(bf16[128,1024]{1,0:T(8,128)(2,1)} %param.2) | copy-start | bytes 786436
  350.0 11.7 %all-to-all-start.1 = ((bf16[128,8,128]{2,0,1:T(8,128)(2,1)}), bf16[128,8,128]{2,0,1:T(8,128)(2,1)S(1)}, u32[]{:S(2)}, u32[]{:S(2)}) async-start(bf16[128,8,128]{2,0,1:T(8,128)(2,1)} %copy_bitcast_fusion.1), calls=%async_computation.3 | async-start | bytes 524288 | tf_op jit(solution)/shard_map/all_to_all | solution.py:94
Sparse Core Ops, SparseCore 0:
  45.2 55.3 all-gather.4
  102.8 95.5 all-gather.2
  219.8 43.6 reduce-scatter.2
  267.4 79.3 reduce-scatter.4
where the time goes:
time: 371 us; the launch traced here: 370 us
  waiting for transfers between devices  165 us (44%)
  blocking collectives  118 us (32%)
  matrix products  29.9 us (8%)
  local copies, waits for them, and re-layouts  21.2 us (6%)
  between operations  15.6 us (4%)
  other arithmetic  10.8 us (3%)
  starting transfers between devices  9.14 us (2%)
    all_gather x1, waiting for transfers between devices, body(): norm_a = lax.all_gather(local_a, 'sample', axis=0, tiled=True)  80.9 us
    psum x1, blocking collectives, body(): loss = lax.psum(loss_sum, ('sample', 'feat')) / (cols_dev * blocks)  65.5 us
    all_gather x1, waiting for transfers between devices, body(): wide_b = lax.all_gather(source_b, 'feat', axis=1, tiled=True)  53.7 us
    psum x1, blocking collectives, body(): lax.psum((jnp.sum(float_a, axis=0), jnp.sum(float_a * float_a, axis=0), j...  34.9 us
    reduce_scatter x1, waiting for transfers between devices, body(): lax.psum_scatter(lax.dot_general(factor_tile, norm_a, (((0,), (1,)), ((),...  25.1 us
    psum x1, blocking collectives, body(): lax.psum((jnp.sum(row_grad, axis=0), jnp.sum(row_grad * float_local, axis...  17.7 us
    dot_general x1, matrix products, body(): lax.dot_general(factor_tile, norm_a, (((0,), (1,)), ((), ())), preferred_...  12 us
    dot_general x1, matrix products, body(): lax.dot_general(norm_a, moved_b, (((0,), (0,)), ((), ())), preferred_elem...  9.54 us
  transfers between devices with their start and end apart: 6, of which 4 were waited for; matrix products, arithmetic and copies ran while one was open for 9% of the time, Pallas kernels for 0%

commit v1 on v0

--- a/solution.py
+++ b/solution.py
@@ -5,6 +5,12 @@
 
 EPSILON = 1e-05
 OFF_WEIGHT = 0.0051
+name_targets = lambda incoming_x, link_axis: jnp.concatenate(
+    lax.all_to_all(
+        jnp.stack(jnp.split(incoming_x, lax.axis_size(link_axis), 1), axis=0), link_axis, 0, 0
+    ),
+    axis=0,
+)
 
 
 def body(view_a, view_b):
@@ -91,7 +97,7 @@
     mean_grad = jnp.mean(col_grad, axis=1, keepdims=True)
     mean_cross = jnp.mean(col_grad * own_t, axis=1, keepdims=True)
     grad_b_t = (scale_b[:, None] * (col_grad - mean_grad - own_t * mean_cross)).astype(jnp.bfloat16)
-    returned = lax.all_to_all(grad_b_t, "sample", split_axis=1, concat_axis=0, tiled=True)
+    returned = name_targets(grad_b_t, "sample")
     grad_b = returned.T
     loss = lax.psum(loss_sum, ("sample", "feat")) / (cols_dev * blocks)
     return (loss, grad_a, grad_b)

time: 371 us -> 375 us (1.011)
  local copies, waits for them, and re-layouts: 21.2 us -> 26.2 us
    unnamed x7 -> x14, local copies, waits for them, and re-layouts: 8.63 us -> 13 us
where the time goes in v1:
time: 375 us; the launch traced here: 374 us
  waiting for transfers between devices  165 us (44%)
  blocking collectives  118 us (31%)
  matrix products  29.9 us (8%)
  local copies, waits for them, and re-layouts  26.2 us (7%)
  between operations  15.7 us (4%)
  other arithmetic  10 us (3%)
  starting transfers between devices  9.14 us (2%)
    all_gather x1, waiting for transfers between devices, body(): norm_a = lax.all_gather(local_a, 'sample', axis=0, tiled=True)  80.9 us
    psum x1, blocking collectives, body(): loss = lax.psum(loss_sum, ('sample', 'feat')) / (cols_dev * blocks)  65.5 us
    all_gather x1, waiting for transfers between devices, body(): wide_b = lax.all_gather(source_b, 'feat', axis=1, tiled=True)  53.7 us
    psum x1, blocking collectives, body(): lax.psum((jnp.sum(float_a, axis=0), jnp.sum(float_a * float_a, axis=0), j...  34.9 us
    reduce_scatter x1, waiting for transfers between devices, body(): lax.psum_scatter(lax.dot_general(factor_tile, norm_a, (((0,), (1,)), ((),...  25.1 us
    psum x1, blocking collectives, body(): lax.psum((jnp.sum(row_grad, axis=0), jnp.sum(row_grad * float_local, axis...  17.7 us
    unnamed x14, local copies, waits for them, and re-layouts  13 us
    dot_general x1, matrix products, body(): lax.dot_general(factor_tile, norm_a, (((0,), (1,)), ((), ())), preferred_...  12 us
  transfers between devices with their start and end apart: 6, of which 4 were waited for; matrix products, arithmetic and copies ran while one was open for 9% of the time, Pallas kernels for 0%

profile of v1, /device:TPU:0, one launch (start us, length us, event | category | flops | bytes accessed | tf_op | source)
XLA Modules:
  0.0 374.5 jit_solution(5703458313522905331)
XLA Ops:
  7.2 0.0 all-gather.5.cloned.1.call-start
  7.2 1.2 convert_reduce_fusion.2
  8.4 34.9 %all-reduce.1 = (f32[1024]{0:T(1024)S(1)}, f32[1024]{0:T(1024)S(1)}, f32[1024]{0:T(1024)S(1)}, f32[1024]{0:T(1024)S(1)}) all-reduce(f32[1024]{0:T(1024)S(1)} %get-tuple-element.23, f32[1024]{0:T(1024)S(1)} %get-tuple-element.24, f32[1024]{0:T(1024)S(1)} %get-tuple-element.8, ...), channel_id=1, replica_groups=mesh['sample'=8,'feat'=16] {'sample'}, use_global_device_ids=true, to_apply=%region_3.0 | all-reduce | flops 4096 | bytes 32768 | tf_op jit(solution)/shard_map/psum | solution.py:27
  43.4 1.7 fusion.8
  45.1 0.0 all-gather.5.cloned.1.call-update
  45.1 0.0 all-gather.3.cloned.1.call-start
  45.2 1.7 fusion.5
  46.9 0.0 all-gather.3.cloned.1.call-update
  46.9 53.7 %all-gather.5.cloned.1.call-done = bf16[128,16384]{1,0:T(8,128)(2,1)} async-done(((bf16[128,1024]{1,0:T(8,128)(2,1)}), bf16[128,16384]{1,0:T(8,128)(2,1)}) %all-gather.5.cloned.1.call-update) | async-done | bytes 4194320 | tf_op jit(solution)/shard_map/all_gather | solution.py:45
  100.6 5.4 %copy.11 = bf16[16,8,128,128]{3,2,1,0:T(8,128)(2,1)} copy(bf16[16,8,128,128]{3,1,2,0:T(8,128)(2,1)} %bitcast.65) | data formatting | bytes 8388608
  106.0 6.9 %copy.7 = bf16[128,16,8,128]{0,3,1,2:T(8,128)(2,1)} copy(bf16[128,16,8,128]{3,2,1,0:T(8,128)(2,1)} %bitcast.64) | data formatting | bytes 8388608 | tf_op jit(solution)/shard_map/reshape | solution.py:47
  112.9 4.6 %all-to-all-start = ((bf16[128,8,2048]{0,2,1:T(8,128)(2,1)}), bf16[128,8,2048]{0,2,1:T(8,128)(2,1)}, u32[]{:S(2)}, u32[]{:S(2)}) async-start(bf16[128,8,2048]{0,2,1:T(8,128)(2,1)} %bitcast.63), calls=%async_computation | async-start | bytes 8388608 | tf_op jit(solution)/shard_map/all_to_all | solution.py:51
  117.5 0.0 reduce-scatter.3.cloned.1.call-start
  117.6 80.9 %all-gather.3.cloned.1.call-done = bf16[1024,1024]{1,0:T(8,128)(2,1)} async-done(((bf16[128,1024]{1,0:T(8,128)(2,1)}), bf16[1024,1024]{1,0:T(8,128)(2,1)}) %all-gather.3.cloned.1.call-update) | async-done | bytes 2097168 | tf_op jit(solution)/shard_map/all_gather | solution.py:43
  198.5 0.0 all-to-all-done
  198.5 9.5 %select_reduce_fusion = (f32[]{:T(128)}, f32[1024,2048]{1,0:T(8,128)S(1)}) fusion(s32[2048]{0:T(1024)S(1)} %fusion.30, pred[2048]{0:T(1024)(128)(4,1)S(1)} %fusion.29, bf16[1024,1024]{1,0:T(8,128)(2,1)} %all-gather.3.cloned.1.call-done, bf16[128,8,2048]{0,2,1:T(8,128)(2,1)} %all-to-all-done), kind=kOutput, calls=%fused_computation.1 | convolution fusion | flops 4313841664 | bytes 14690308 | tf_op jit(solution)/shard_map/dot_general | solution.py:55
  208.0 0.0 copy-start.2
  208.0 3.2 copy-done.2
  211.2 0.0 copy-start.1
  211.2 8.4 %convolution_convert_fusion.1 = bf16[1024,1024]{1,0:T(8,128)(2,1)} fusion(f32[1024,2048]{1,0:T(8,128)S(1)} %get-tuple-element.22, s32[2048]{0:T(1024)S(1)} %fusion.30, pred[2048]{0:T(1024)(128)(4,1)S(1)} %fusion.29, bf16[128,8,2048]{0,2,1:T(8,128)(2,1)} %all-to-all-done), kind=kOutput, calls=%fused_computation.6 | convolution fusion | flops 4310695936 | bytes 14690304 | tf_op jit(solution)/shard_map/dot_general | solution.py:73
  219.7 0.0 reduce-scatter.3.cloned.1.call-update
  219.7 0.0 reduce-scatter.5.cloned.1.call-start
  219.7 0.0 copy-done.1
  219.7 12.0 %convolution_convert_fusion = bf16[2048,1024]{1,0:T(8,128)(2,1)} fusion(bf16[1024,1024]{1,0:T(8,128)(2,1)S(1)} %copy-done.1, f32[1024,2048]{1,0:T(8,128)} %copy-done.2, s32[2048]{0:T(1024)S(1)} %fusion.30, pred[2048]{0:T(1024)(128)(4,1)S(1)} %fusion.29), kind=kOutput, calls=%fused_computation.5 | convolution fusion | flops 4311744512 | bytes 14690304 | tf_op jit(solution)/shard_map/dot_general | solution.py:89
  231.7 0.0 reduce-scatter.5.cloned.1.call-update
  231.7 0.1 dynamic_slice.6
  231.8 65.5 %psum.53 = f32[]{:T(128)} all-reduce(f32[]{:T(128)} %get-tuple-element.21), channel_id=1, replica_groups=mesh['sample'=8,'feat'=16] {'sample','feat'}, use_global_device_ids=true, to_apply=%region_9.10 | all-reduce | flops 1 | bytes 8 | tf_op jit(solution)/shard_map/psum | solution.py:102
  298.0 0.0 copy-start
  298.0 4.8 %copy_bitcast_fusion = bf16[1024,2048]{0,1:T(8,128)(2,1)} fusion(bf16[128,8,2048]{0,2,1:T(8,128)(2,1)} %all-to-all-done), kind=kLoop, calls=%fused_computation.4 | loop fusion | bytes 8388608 | tf_op jit(solution)/shard_map/all_to_all | solution.py:51
  302.8 0.0 reduce-scatter.3.cloned.1.call-done
  302.8 0.0 copy-done
  302.8 1.1 convert_reduce_fusion.1
  303.9 17.7 %all-reduce = (f32[1024]{0:T(1024)S(1)}, f32[1024]{0:T(1024)S(1)}) all-reduce(f32[1024]{0:T(1024)S(1)} %get-tuple-element.6, f32[1024]{0:T(1024)S(1)} %get-tuple-element.5), channel_id=1, replica_groups=mesh['sample'=8,'feat'=16] {'sample'}, use_global_device_ids=true, to_apply=%region_14.15 | all-reduce | flops 2048 | bytes 16384 | tf_op jit(solution)/shard_map/psum | solution.py:82
  321.7 25.1 %reduce-scatter.5.cloned.1.call-done = bf16[128,1024]{1,0:T(8,128)(2,1)} async-done(((bf16[2048,1024]{1,0:T(8,128)(2,1)}), bf16[128,1024]{1,0:T(8,128)(2,1)}) %reduce-scatter.5.cloned.1.call-update) | async-done | bytes 262160 | tf_op jit(solution)/shard_map/reduce_scatter | solution.py:88
  346.8 1.2 convert_reduce_fusion
  348.0 1.3 fusion.13
  349.3 0.6 fusion.22
  349.9 0.6 fusion.21
  350.5 0.6 fusion.20
  351.2 0.6 fusion.19
  351.8 0.6 fusion.18
  352.4 0.6 fusion.17
  353.0 0.6 fusion.16
  353.7 0.6 fusion.15
  354.3 4.4 %all-to-all-start.1 = ((bf16[8,128,128]{2,1,0:T(8,128)(2,1)}), bf16[8,128,128]{2,1,0:T(8,128)(2,1)S(1)}, u32[]{:S(2)}, u32[]{:S(2)}) async-start(bf16[8,128,128]{2,1,0:T(8,128)(2,1)} %fusion.15), calls=%async_computation.3 | async-start | bytes 524288 | tf_op jit(solution)/shard_map/all_to_all | solution.py:9
  358.7 1.8 fusion.3
  360.5 5.5 %all-to-all-done.1 = bf16[8,128,128]{2,1,0:T(8,128)(2,1)S(1)} async-done(((bf16[8,128,128]{2,1,0:T(8,128)(2,1)}), bf16[8,128,128]{2,1,0:T(8,128)(2,1)S(1)}, u32[]{:S(2)}, u32[]{:S(2)}) %all-to-all-start.1) | async-done | bytes 262176 | tf_op jit(solution)/shard_map/all_to_all | solution.py:9
  366.0 0.8 copy.9
  (8 shorter events, 0.1 us)
Async XLA Ops:
  7.2 93.5 %all-gather.5.cloned.1.call-start = ((), (), s32[]{:S(2)}) async-start(), calls=%async_computation.5 | async-start | bytes 4456448 | tf_op jit(solution)/shard_map/all_gather | solution.py:45
  45.1 153.4 %all-gather.3.cloned.1.call-start = ((), (), s32[]{:S(2)}) async-start(), calls=%async_computation.4 | async-start | bytes 2359296 | tf_op jit(solution)/shard_map/all_gather | solution.py:43
  112.9 85.6 %all-to-all-start = ((bf16[128,8,2048]{0,2,1:T(8,128)(2,1)}), bf16[128,8,2048]{0,2,1:T(8,128)(2,1)}, u32[]{:S(2)}, u32[]{:S(2)}) async-start(bf16[128,8,2048]{0,2,1:T(8,128)(2,1)} %bitcast.63), calls=%async_computation | async-start | bytes 8388608 | tf_op jit(solution)/shard_map/all_to_all | solution.py:51
  117.5 185.3 %reduce-scatter.3.cloned.1.call-start = ((), (), s32[]{:S(2)}) async-start(), calls=%async_computation.6 | async-start | bytes 2359296 | tf_op jit(solution)/shard_map/reduce_scatter | solution.py:78
  208.0 3.2 copy-start.2
  211.2 8.5 %copy-start.1 = (bf16[1024,1024]{1,0:T(8,128)(2,1)S(1)}, bf16[1024,1024]{1,0:T(8,128)(2,1)}, u32[]{:S(2)}) copy-start(bf16[1024,1024]{1,0:T(8,128)(2,1)} %all-gather.3.cloned.1.call-done) | copy-start | bytes 6291460
  219.7 127.1 %reduce-scatter.5.cloned.1.call-start = ((), (), s32[]{:S(2)}) async-start(), calls=%async_computation.7 | async-start | bytes 4456448 | tf_op jit(solution)/shard_map/reduce_scatter | solution.py:88
  298.0 4.8 %copy-start = (bf16[128,1024]{1,0:T(8,128)(2,1)S(1)}, bf16[128,1024]{1,0:T(8,128)(2,1)}, u32[]{:S(2)}) copy-start(bf16[128,1024]{1,0:T(8,128)(2,1)} %param.2) | copy-start | bytes 786436
  354.3 11.7 %all-to-all-start.1 = ((bf16[8,128,128]{2,1,0:T(8,128)(2,1)}), bf16[8,128,128]{2,1,0:T(8,128)(2,1)S(1)}, u32[]{:S(2)}, u32[]{:S(2)}) async-start(bf16[8,128,128]{2,1,0:T(8,128)(2,1)} %fusion.15), calls=%async_computation.3 | async-start | bytes 524288 | tf_op jit(solution)/shard_map/all_to_all | solution.py:9
Sparse Core Ops, SparseCore 0:
  45.2 55.3 all-gather.4
  102.8 95.5 all-gather.2
  219.8 43.6 reduce-scatter.2
  267.4 79.3 reduce-scatter.4
